TPU v7x, 1024 devices: a whole 8x8x8 slice. The times are simulated.
1024 devices in a mesh: pipe: 8 (over y), seq: 16 (over z, core), head: 8 (over x).
Axes of the slice: x: 8, y: 8, z: 8, core: 2. Of those that a mesh axis runs over, the one named last changes fastest.
Arguments:
- queries: bfloat16 [8, 4096, 4096], P('pipe', 'seq', 'head'), may hold values from -6 to 6
- keys: bfloat16 [8, 4096, 4096], P('pipe', 'seq', 'head'), may hold values from -6 to 6
- values: bfloat16 [8, 4096, 4096], P('pipe', 'seq', 'head'), may hold values from -6 to 6
- output_gradient: bfloat16 [8, 4096, 4096], P('pipe', 'seq', 'head'), may hold values from -0.019897461 to 0.019897461
- log_decay: float32 [8, 32, 4096], P('pipe', 'head', 'seq'), may hold values from -1.5 to 0
Outputs:
- query_grad_in: bfloat16 [8, 4096, 4096], P('pipe', 'seq', 'head')
- key_grad_in: bfloat16 [8, 4096, 4096], P('pipe', 'seq', 'head')
- value_grad_in: bfloat16 [8, 4096, 4096], P('pipe', 'seq', 'head')
All inputs are finite; a program needn't handle non-finite values.
Results may differ from a plain program's by a relative error of at most 0.0057.
Values may be sent and summed in bfloat16 or wider, within the bound.
A program may use at most 32 MiB of HBM per device.

v0:
```python
import jax
import jax.numpy as jnp
from jax import lax
from jax.sharding import PartitionSpec as P


def shifted(block, axis, distance):
    devices = range(lax.axis_size(axis))
    route = [(i - distance, i) for i in devices if i - distance in devices]
    return lax.ppermute(block, axis, route)


def segment_states(queries, keys, values, output_gradient, cum):
    total = cum[:, -1]
    scaled_keys = (jnp.exp(total[:, None] - cum)[..., None] * keys).astype(jnp.bfloat16)
    scaled_queries = (jnp.exp(cum)[..., None] * queries).astype(jnp.bfloat16)
    local_forward_state = jnp.einsum(
        "nwd,nws->nds", scaled_keys, values, preferred_element_type=jnp.float32
    )
    local_reverse_state = jnp.einsum(
        "nwd,nws->nds", scaled_queries, output_gradient, preferred_element_type=jnp.float32
    )
    return (total, local_forward_state, local_reverse_state)


def head_grads(inputs):
    queries, keys, values, output_gradient, cum, total, state_in, state_rev = inputs
    count = cum.shape[0]
    later = lax.broadcasted_iota(jnp.int32, (count, count), 0) >= lax.broadcasted_iota(
        jnp.int32, (count, count), 1
    )
    decay = jnp.where(later, jnp.exp(jnp.where(later, cum[:, None] - cum[None, :], 0.0)), 0.0)
    inner = (((1,), (1,)), ((), ()))
    outer = (((0,), (0,)), ((), ()))
    pair = (
        lax.dot_general(output_gradient, values, inner, preferred_element_type=jnp.float32) * decay
    ).astype(jnp.bfloat16)
    score = (
        lax.dot_general(queries, keys, inner, preferred_element_type=jnp.float32) * decay
    ).astype(jnp.bfloat16)
    forward_b = state_in.astype(jnp.bfloat16)
    reverse_b = state_rev.astype(jnp.bfloat16)
    lead = jnp.exp(cum)[:, None]
    tail = jnp.exp(total - cum)[:, None]
    query_grad = jnp.dot(pair, keys, preferred_element_type=jnp.float32) + lead * lax.dot_general(
        output_gradient, forward_b, inner, preferred_element_type=jnp.float32
    )
    key_grad = lax.dot_general(
        pair, queries, outer, preferred_element_type=jnp.float32
    ) + tail * lax.dot_general(values, reverse_b, inner, preferred_element_type=jnp.float32)
    value_grad = lax.dot_general(
        score, output_gradient, outer, preferred_element_type=jnp.float32
    ) + tail * jnp.dot(keys, reverse_b, preferred_element_type=jnp.float32)
    return (
        query_grad.astype(jnp.bfloat16),
        key_grad.astype(jnp.bfloat16),
        value_grad.astype(jnp.bfloat16),
    )


def per_device(queries, keys, values, output_gradient, log_decay):
    length = queries.shape[1]
    head_count = log_decay.shape[1]
    head_size = queries.shape[2] // head_count

    def split(array):
        return array[0].reshape(length, head_count, head_size).transpose(1, 0, 2)

    parts = (split(queries), split(keys), split(values), split(output_gradient))
    cum = jnp.cumsum(log_decay[0], axis=1)
    total, local_forward_state, local_reverse_state = segment_states(
        parts[0], parts[1], parts[2], parts[3], cum
    )
    everyone = lax.all_gather(total[None], "seq", axis=0, tiled=True)
    through = jnp.cumsum(everyone, axis=0)
    before = through - everyone
    position = lax.axis_index("seq")
    mine_before = lax.dynamic_slice_in_dim(before, position, 1, 0)
    mine_through = lax.dynamic_slice_in_dim(through, position, 1, 0)
    piece_list = (
        lax.all_gather(local_forward_state[None], "seq", axis=0, tiled=True),
        lax.all_gather(local_reverse_state[None], "seq", axis=0, tiled=True),
    )
    count = piece_list[0].shape[0]
    order = jnp.arange(count, dtype=jnp.int32)
    incoming_weight = jnp.where(
        (order < position)[:, None], jnp.exp(jnp.minimum(mine_before - through, 0.0)), 0.0
    )
    reverse_weight = jnp.where(
        (order > position)[:, None], jnp.exp(jnp.minimum(before - mine_through, 0.0)), 0.0
    )
    forward_total_state = jnp.einsum(
        "mi,miuj->iuj", incoming_weight, piece_list[0], precision=lax.Precision.HIGHEST
    )
    reverse_total_state = jnp.einsum(
        "mi,miuj->iuj", reverse_weight, piece_list[1], precision=lax.Precision.HIGHEST
    )

    def merge(array):
        return array.transpose(1, 0, 2).reshape(length, head_count * head_size)

    query_grad, key_grad, value_grad = lax.map(
        head_grads, parts + (cum, total, forward_total_state, reverse_total_state)
    )
    passed = shifted((merge(query_grad), merge(key_grad), merge(value_grad)), "pipe", -1)
    return (passed[0][None], passed[1][None], passed[2][None])


def solution(mesh):
    in_specs = (
        P("pipe", "seq", "head"),
        P("pipe", "seq", "head"),
        P("pipe", "seq", "head"),
        P("pipe", "seq", "head"),
        P("pipe", "head", "seq"),
    )
    out_specs = (P("pipe", "seq", "head"), P("pipe", "seq", "head"), P("pipe", "seq", "head"))
    return jax.shard_map(
        per_device, mesh=mesh, in_specs=in_specs, out_specs=out_specs, check_vma=False
    )
```

profile of v0, /device:TPU:1, one launch (start us, length us, event | category | flops | bytes accessed | tf_op | source)
XLA Modules:
  0.0 173.1 jit_solution(1259726008891780788)
XLA Ops:
  7.2 0.7 reshape.84
  7.9 1.2 reduce-window.6
  9.8 1.1 copy.34
  10.9 1.1 copy.31
  12.0 0.9 fusion.58
  13.0 1.1 copy.36
  14.1 1.1 copy.30
  15.2 0.9 fusion.59
  16.2 1.2 dynamic-slice
  18.2 37.0 %all-reduce = f32[64]{0:T(128)S(1)} all-reduce(f32[64]{0:T(128)S(1)} %dynamic-update-slice), channel_id=2, replica_groups=mesh['pipe'=8,'seq'=16,'head'=8] {'seq'}, use_global_device_ids=true, to_apply=%add | all-reduce | flops 64 | bytes 512
  55.8 18.8 %all-gather.6.cloned.1.call-done = f32[64,128,128]{2,1,0:T(8,128)} async-done(((f32[4,128,128]{2,1,0:T(8,128)}), f32[64,128,128]{2,1,0:T(8,128)}) %all-gather.6.cloned.1.call-update) | async-done | bytes 4194320 | tf_op jit(solution)/shard_map/all_gather | solution.py:81
  74.5 6.4 %fusion.56 = f32[4,1,128,128]{3,1,2,0:T(1,128)S(1)} fusion(f32[16,4,1,1]{0,2,3,1:T(1,128)S(1)} %copy.46, f32[16,4,128,128]{3,2,1,0:T(8,128)} %bitcast.163), kind=kOutput, calls=%fused_computation.61 | convolution fusion | flops 12582912 | bytes 4456704 | tf_op jit(solution)/shard_map/mi,miuj->iuj/dot_general | solution.py:92
  81.0 43.8 %all-gather.8.cloned.1.call-done = f32[64,128,128]{2,1,0:T(8,128)} async-done(((f32[4,128,128]{2,1,0:T(8,128)}), f32[64,128,128]{2,1,0:T(8,128)}) %all-gather.8.cloned.1.call-update) | async-done | bytes 4194320 | tf_op jit(solution)/shard_map/all_gather | solution.py:82
  124.8 6.4 %fusion.54 = f32[4,1,128,128]{3,1,2,0:T(1,128)S(1)} fusion(f32[16,4,1,1]{0,2,3,1:T(1,128)S(1)} %copy.50, f32[16,4,128,128]{3,2,1,0:T(8,128)} %bitcast.164), kind=kOutput, calls=%fused_computation.59 | convolution fusion | flops 12582912 | bytes 4456704 | tf_op jit(solution)/shard_map/mi,miuj->iuj/dot_general | solution.py:95
  131.2 12.1 %while.14 = (s32[]{:T(128)}, bf16[4,256,128]{2,1,0:T(8,128)(2,1)S(1)}, bf16[4,256,128]{2,1,0:T(8,128)(2,1)S(1)}, bf16[4,256,128]{2,1,0:T(8,128)(2,1)S(1)}, bf16[...) while((s32[]{:T(128)}, ...), condition=%wide.region_4.5_spmd, body=%wide.region_3.4_spmd.sunk | while | flops 110133504 | bytes 2150553 | solution.py:102
  143.4 1.3 collective-permute-start.1
  144.7 1.3 collective-permute-start
  146.1 1.3 collective-permute-start.2
  147.4 5.5 %collective-permute-done.1 = bf16[256,512]{1,0:T(8,128)(2,1)S(1)} collective-permute-done((bf16[256,512]{1,0:T(8,128)(2,1)S(1)}, bf16[256,512]{1,0:T(8,128)(2,1)S(1)}, u32[]{:S(2)}, u32[]{:S(2)}) %collective-permute-start.1) | collective-permute-done | bytes 262176 | tf_op jit(solution)/shard_map/ppermute | solution.py:10
  152.9 5.6 %collective-permute-done = bf16[256,512]{1,0:T(8,128)(2,1)S(1)} collective-permute-done((bf16[256,512]{1,0:T(8,128)(2,1)S(1)}, bf16[256,512]{1,0:T(8,128)(2,1)S(1)}, u32[]{:S(2)}, u32[]{:S(2)}) %collective-permute-start) | collective-permute-done | bytes 262176 | tf_op jit(solution)/shard_map/ppermute | solution.py:10
  158.5 5.6 %collective-permute-done.2 = bf16[256,512]{1,0:T(8,128)(2,1)S(1)} collective-permute-done((bf16[256,512]{1,0:T(8,128)(2,1)S(1)}, bf16[256,512]{1,0:T(8,128)(2,1)S(1)}, u32[]{:S(2)}, u32[]{:S(2)}) %collective-permute-start.2) | collective-permute-done | bytes 262176 | tf_op jit(solution)/shard_map/ppermute | solution.py:10
  164.1 0.7 copy.95
  164.8 0.7 copy.96
  165.5 0.7 copy.97
  (72 shorter events, 13.5 us)
Async XLA Ops:
  7.2 67.4 %all-gather.6.cloned.1.call-start = ((), (), s32[]{:S(2)}) async-start(), calls=%async_computation | async-start | bytes 4456448 | tf_op jit(solution)/shard_map/all_gather | solution.py:81
  12.9 111.8 %all-gather.8.cloned.1.call-start = ((), (), s32[]{:S(2)}) async-start(), calls=%async_computation.1 | async-start | bytes 4456448 | tf_op jit(solution)/shard_map/all_gather | solution.py:82
  143.4 9.5 %collective-permute-start.1 = (bf16[256,512]{1,0:T(8,128)(2,1)S(1)}, bf16[256,512]{1,0:T(8,128)(2,1)S(1)}, u32[]{:S(2)}, u32[]{:S(2)}) collective-permute-start(bf16[256,512]{1,0:T(8,128)(2,1)S(1)} %copy_bitcast_fusion.1), channel_id=1, source_target_pairs={{128,0},{256,128},{384,256},{512,384},{640,512},{768,640},{896,768... | collective-permute-start | bytes 786440 | tf_op jit(solution)/shard_map/ppermute | solution.py:10
  144.7 13.8 %collective-permute-start = (bf16[256,512]{1,0:T(8,128)(2,1)S(1)}, bf16[256,512]{1,0:T(8,128)(2,1)S(1)}, u32[]{:S(2)}, u32[]{:S(2)}) collective-permute-start(bf16[256,512]{1,0:T(8,128)(2,1)S(1)} %copy_bitcast_fusion.2), channel_id=1, source_target_pairs={{128,0},{256,128},{384,256},{512,384},{640,512},{768,640},{896,768... | collective-permute-start | bytes 786440 | tf_op jit(solution)/shard_map/ppermute | solution.py:10
  146.1 18.1 %collective-permute-start.2 = (bf16[256,512]{1,0:T(8,128)(2,1)S(1)}, bf16[256,512]{1,0:T(8,128)(2,1)S(1)}, u32[]{:S(2)}, u32[]{:S(2)}) collective-permute-start(bf16[256,512]{1,0:T(8,128)(2,1)S(1)} %copy_bitcast_fusion), channel_id=1, source_target_pairs={{128,0},{256,128},{384,256},{512,384},{640,512},{768,640},{896,768... | collective-permute-start | bytes 786440 | tf_op jit(solution)/shard_map/ppermute | solution.py:10
Sparse Core Ops, SparseCore 0:
  13.1 61.4 all-gather.5
  77.8 46.9 all-gather.7
where the time goes:
time: 174 us; the launch traced here: 173 us
  waiting for transfers between devices  79.4 us (46%)
  blocking collectives  37 us (21%)
  matrix products  21.7 us (12%)
  between operations  14.8 us (9%)
  local copies, waits for them, and re-layouts  11.8 us (7%)
  other arithmetic  4.22 us (2%)
  starting transfers between devices  3.96 us (2%)
    all_gather x1, waiting for transfers between devices, per_device(): lax.all_gather(local_reverse_state[None], 'seq', axis=0, tiled=True)  43.8 us
    unnamed x1, blocking collectives  37 us
    all_gather x1, waiting for transfers between devices, per_device(): lax.all_gather(local_forward_state[None], 'seq', axis=0, tiled=True)  18.8 us
    ppermute x3, waiting for transfers between devices, shifted(): return lax.ppermute(block, axis, route)  16.8 us
    unnamed x11, local copies, waits for them, and re-layouts  7.95 us
    dot_general x1, matrix products, per_device(): jnp.einsum('mi,miuj->iuj', incoming_weight, piece_list[0], precision=lax....  6.42 us
    dot_general x1, matrix products, per_device(): jnp.einsum('mi,miuj->iuj', reverse_weight, piece_list[1], precision=lax.P...  6.42 us
    ppermute x3, starting transfers between devices, shifted(): return lax.ppermute(block, axis, route)  3.88 us
  transfers between devices with their start and end apart: 5, of which 5 were waited for; matrix products, arithmetic and copies ran while one was open for 7% of the time, Pallas kernels for 0%

commit v1 on v0

v1 whole, which is shorter than its diff:
```python
import functools

import jax
import jax.numpy as jnp
from jax import lax
from jax.experimental import pallas as pl
from jax.experimental.pallas import tpu as pltpu
from jax.sharding import PartitionSpec as P

MESH = pl.DeviceIdType.MESH
INNER = (((1,), (1,)), ((), ()))
OUTER = (((0,), (0,)), ((), ()))
F32 = jnp.float32
BF16 = jnp.bfloat16


def mm(a, b):
    return jnp.dot(a, b, preferred_element_type=F32)


def mm_nt(a, b):
    return lax.dot_general(a, b, INNER, preferred_element_type=F32)


def mm_tn(a, b):
    return lax.dot_general(a, b, OUTER, preferred_element_type=F32)


def far_first(count):
    ring = count + 1
    return sorted(range(1, count + 1), key=lambda d: -min(d, ring - d))


def kernel(
    n_pipe,
    n_chip,
    q_hbm,
    k_hbm,
    v_hbm,
    g_hbm,
    ld_hbm,
    oq_ref,
    ok_ref,
    ov_ref,
    q_ref,
    k_ref,
    v_ref,
    g_ref,
    ld_ref,
    part_ref,
    cum_ref,
    col_ref,
    lead_ref,
    tail_ref,
    tot_ref,
    tot_sib_ref,
    chip_tot_ref,
    far_tot_ref,
    weight_ref,
    local_ref,
    sib_state_ref,
    agg_ref,
    far_ref,
    own_ref,
    sib_sum_ref,
    state_ref,
    iq_ref,
    ik_ref,
    iv_ref,
    out_ref,
    zero_ref,
    in_sem,
    tot_send,
    tot_recv,
    x_send,
    x_recv,
    ft_send,
    ft_recv,
    agg_send,
    agg_recv,
    u_send,
    u_recv,
    y_send,
    y_recv,
    zero_sem,
):
    length, width = q_ref.shape
    heads = ld_ref.shape[1]
    size = width // heads
    half = length // 2
    n_far = n_chip - 1

    pipe = lax.axis_index("pipe")
    seq = lax.axis_index("seq")
    chip = lax.div(seq, 2)
    core = lax.rem(seq, 2)
    sibling = seq + 1 - 2 * core
    step = 2 * core - 1
    n_partner = core * (n_far - chip) + (1 - core) * chip
    below = lax.rem(pipe + n_pipe - 1, n_pipe)
    above = lax.rem(pipe + 1, n_pipe)

    def partner(d):
        return 2 * (chip + step * d) + (1 - core)

    barrier = pltpu.get_barrier_semaphore()
    pl.semaphore_signal(barrier, inc=1, device_id={"seq": sibling}, device_id_type=MESH)
    for d in far_first(n_far):

        @pl.when(d <= n_partner)
        def _():
            pl.semaphore_signal(barrier, inc=1, device_id={"seq": partner(d)}, device_id_type=MESH)

    @pl.when(pipe < n_pipe - 1)
    def _():
        pl.semaphore_signal(barrier, inc=1, device_id={"pipe": above}, device_id_type=MESH)

    loads = [
        pltpu.make_async_copy(ld_hbm, ld_ref, in_sem.at[0]),
        pltpu.make_async_copy(k_hbm.at[0], k_ref, in_sem.at[1]),
        pltpu.make_async_copy(v_hbm.at[0], v_ref, in_sem.at[2]),
        pltpu.make_async_copy(q_hbm.at[0], q_ref, in_sem.at[3]),
        pltpu.make_async_copy(g_hbm.at[0], g_ref, in_sem.at[4]),
    ]
    for load in loads:
        load.start()

    for d in range(1, n_far + 1):

        @pl.when(d > n_partner)
        def _():
            far_ref[d - 1] = jnp.zeros(far_ref.shape[1:], BF16)
            far_tot_ref[d - 1] = jnp.zeros(far_tot_ref.shape[1:], F32)

    part_ref[...] = jnp.zeros_like(part_ref)
    cum_ref[...] = jnp.zeros_like(cum_ref)

    @pl.when(pipe == n_pipe - 1)
    def _():
        zero_ref[...] = jnp.zeros_like(zero_ref)
        clears = [
            pltpu.make_async_copy(zero_ref, o.at[0], zero_sem.at[i])
            for i, o in enumerate((oq_ref, ok_ref, ov_ref))
        ]
        for clear in clears:
            clear.start()
        for clear in clears:
            clear.wait()

    loads[0].wait()
    ld = ld_ref[0]
    high = ld.astype(BF16).astype(F32)
    rest = ld - high
    middle = rest.astype(BF16).astype(F32)
    part_ref[0:heads, :] = high
    part_ref[heads : 2 * heads, :] = middle
    part_ref[2 * heads : 3 * heads, :] = rest - middle
    earlier = (
        lax.broadcasted_iota(jnp.int32, (length, length), 0)
        <= lax.broadcasted_iota(jnp.int32, (length, length), 1)
    ).astype(F32).astype(BF16)
    sums = mm(part_ref[...].astype(BF16), earlier)
    cum_ref[0:heads, :] = sums[0:heads] + sums[heads : 2 * heads] + sums[2 * heads : 3 * heads]
    tot_ref[...] = jnp.broadcast_to(cum_ref[:, length - 1 : length], tot_ref.shape)

    for load in loads[1:]:
        load.wait()

    def cols(ref, h):
        return ref[:, h * size : (h + 1) * size]

    for h in range(heads):
        for b in range(2):
            rows = slice(b * half, (b + 1) * half)
            row = jnp.broadcast_to(cum_ref[h : h + 1, rows], (half, half))
            col_ref[h, rows, :] = row.T
        col = col_ref[h]
        lead = jnp.exp(col)
        tail = jnp.exp(tot_ref[h : h + 1, :] - col)
        lead_ref[h] = lead
        tail_ref[h] = tail
        key_weighted = (tail * cols(k_ref, h).astype(F32)).astype(BF16)
        query_weighted = (lead * cols(q_ref, h).astype(F32)).astype(BF16)
        local_ref[0, h] = mm_tn(key_weighted, cols(v_ref, h))
        local_ref[1, h] = mm_tn(query_weighted, cols(g_ref, h))
        if h == 0:
            pl.semaphore_wait(barrier, 1 + n_partner + jnp.minimum(pipe, 1))
            tot_copy = pltpu.make_async_remote_copy(
                src_ref=tot_ref,
                dst_ref=tot_sib_ref,
                send_sem=tot_send.at[0],
                recv_sem=tot_recv.at[0],
                device_id={"seq": sibling},
                device_id_type=MESH,
            )
            tot_copy.start()
        x_copy(local_ref, sib_state_ref, core, h, x_send, x_recv, sibling).start()

    def tot_far(d):
        return pltpu.make_async_remote_copy(
            src_ref=chip_tot_ref,
            dst_ref=far_tot_ref.at[d - 1],
            send_sem=ft_send.at[d - 1],
            recv_sem=ft_recv.at[d - 1],
            device_id={"seq": partner(d)},
            device_id_type=MESH,
        )

    def agg_far(d, h):
        return pltpu.make_async_remote_copy(
            src_ref=agg_ref.at[h],
            dst_ref=far_ref.at[d - 1, h],
            send_sem=agg_send.at[d - 1, h],
            recv_sem=agg_recv.at[d - 1, h],
            device_id={"seq": partner(d)},
            device_id_type=MESH,
        )

    tot_copy.wait_recv()
    chip_tot_ref[...] = tot_ref[...] + tot_sib_ref[...]
    for d in far_first(n_far):

        @pl.when(d <= n_partner)
        def _():
            tot_far(d).start()

    for h in range(heads):
        x_copy(local_ref, sib_state_ref, core, h, x_send, x_recv, sibling).wait_recv()
        agg_ref[h] = (
            jnp.exp(tot_ref[h : h + 1, :]) * sib_state_ref[h] + local_ref[1 - core, h]
        ).astype(BF16)
        for d in far_first(n_far):

            @pl.when(d <= n_partner)
            def _():
                agg_far(d, h).start()

    at = lax.broadcasted_iota(jnp.int32, (half, half), 0)
    by = lax.broadcasted_iota(jnp.int32, (half, half), 1)
    lower, upper = at >= by, at <= by
    for h in range(heads):
        q, k, v, g = cols(q_ref, h), cols(k_ref, h), cols(v_ref, h), cols(g_ref, h)
        row0, row1 = cum_ref[h : h + 1, :half], cum_ref[h : h + 1, half:]
        col0, col1 = col_ref[h, :half, :], col_ref[h, half:, :]
        d00 = jnp.where(lower, jnp.exp(col0 - row0), 0.0)
        d10 = jnp.exp(col1 - row0)
        d11 = jnp.where(lower, jnp.exp(col1 - row1), 0.0)
        pair0 = (mm_nt(g[:half], v[:half]) * d00).astype(BF16)
        pair1 = (mm_nt(g[half:], v) * jnp.concatenate([d10, d11], axis=1)).astype(BF16)
        iq_ref[h, :half, :] = mm(pair0, k[:half])
        iq_ref[h, half:, :] = mm(pair1, k)
        e00 = jnp.where(upper, jnp.exp(row0 - col0), 0.0)
        e01 = jnp.exp(row1 - col0)
        e11 = jnp.where(upper, jnp.exp(row1 - col1), 0.0)
        e0 = jnp.concatenate([e00, e01], axis=1)
        pair_t0 = (mm_nt(v[:half], g) * e0).astype(BF16)
        pair_t1 = (mm_nt(v[half:], g[half:]) * e11).astype(BF16)
        ik_ref[h, :half, :] = mm(pair_t0, q)
        ik_ref[h, half:, :] = mm(pair_t1, q[half:])
        score_t0 = (mm_nt(k[:half], q) * e0).astype(BF16)
        score_t1 = (mm_nt(k[half:], q[half:]) * e11).astype(BF16)
        iv_ref[h, :half, :] = mm(score_t0, g)
        iv_ref[h, half:, :] = mm(score_t1, g[half:])

    between = jnp.zeros(tot_ref.shape, F32)
    for d in range(1, n_far + 1):

        @pl.when(d <= n_partner)
        def _():
            tot_far(d).wait_recv()

        weight_ref[d - 1] = jnp.exp(between)
        between = between + far_tot_ref[d - 1]

    def u_copy(h):
        return pltpu.make_async_remote_copy(
            src_ref=own_ref.at[h],
            dst_ref=sib_sum_ref.at[h],
            send_sem=u_send.at[h],
            recv_sem=u_recv.at[h],
            device_id={"seq": sibling},
            device_id_type=MESH,
        )

    outs = (oq_ref, ok_ref, ov_ref)

    def y_copy(j, h):
        return pltpu.make_async_remote_copy(
            src_ref=out_ref.at[j, h],
            dst_ref=outs[j].at[0, :, pl.ds(h * size, size)],
            send_sem=y_send.at[j, h],
            recv_sem=y_recv.at[j, h],
            device_id={"pipe": below},
            device_id_type=MESH,
        )

    def send_down(j, h):
        @pl.when(pipe > 0)
        def _():
            y_copy(j, h).start()

    for h in range(heads):
        for d in range(1, n_far + 1):

            @pl.when(d <= n_partner)
            def _():
                agg_far(d, h).wait_recv()

        total = jnp.zeros((size, size), F32)
        for d in range(1, n_far + 1):
            total = total + weight_ref[d - 1, h : h + 1, :] * far_ref[d - 1, h].astype(F32)
        own_ref[h] = total
        u_copy(h).start()
        state_ref[core, h] = total.astype(BF16)
        u_copy(h).wait_recv()
        state_ref[1 - core, h] = (
            jnp.exp(tot_sib_ref[h : h + 1, :]) * sib_sum_ref[h] + sib_state_ref[h]
        ).astype(BF16)
        state_in, state_rev = state_ref[0, h], state_ref[1, h]
        lead, tail = lead_ref[h], tail_ref[h]
        out_ref[0, h] = (iq_ref[h] + lead * mm_nt(cols(g_ref, h), state_in)).astype(BF16)
        send_down(0, h)
        out_ref[1, h] = (ik_ref[h] + tail * mm_nt(cols(v_ref, h), state_rev)).astype(BF16)
        send_down(1, h)
        out_ref[2, h] = (iv_ref[h] + tail * mm(cols(k_ref, h), state_rev)).astype(BF16)
        send_down(2, h)

    tot_copy.wait_send()
    for h in range(heads):
        x_copy(local_ref, sib_state_ref, core, h, x_send, x_recv, sibling).wait_send()
        u_copy(h).wait_send()
    for d in range(1, n_far + 1):

        @pl.when(d <= n_partner)
        def _():
            tot_far(d).wait_send()
            for h in range(heads):
                agg_far(d, h).wait_send()

    @pl.when(pipe > 0)
    def _():
        for h in range(heads):
            for j in range(3):
                y_copy(j, h).wait_send()

    @pl.when(pipe < n_pipe - 1)
    def _():
        for h in range(heads):
            for j in range(3):
                y_copy(j, h).wait_recv()


def x_copy(local_ref, sib_state_ref, core, h, x_send, x_recv, sibling):
    return pltpu.make_async_remote_copy(
        src_ref=local_ref.at[core, h],
        dst_ref=sib_state_ref.at[h],
        send_sem=x_send.at[h],
        recv_sem=x_recv.at[h],
        device_id={"seq": sibling},
        device_id_type=MESH,
    )


def per_device(n_pipe, n_seq, queries, keys, values, output_gradient, log_decay):
    length, width = queries.shape[1:]
    heads = log_decay.shape[1]
    size = width // heads
    n_chip = n_seq // 2
    n_far = n_chip - 1
    dma = pltpu.SemaphoreType.DMA
    tile = (8, size)
    anywhere = pl.BlockSpec(memory_space=pl.ANY)
    return pl.pallas_call(
        functools.partial(kernel, n_pipe, n_chip),
        out_shape=[jax.ShapeDtypeStruct(queries.shape, BF16)] * 3,
        in_specs=[anywhere] * 5,
        out_specs=[anywhere] * 3,
        scratch_shapes=[
            *[pltpu.VMEM((length, width), BF16)] * 4,
            pltpu.VMEM((1, heads, length), F32),
            pltpu.VMEM((16, length), F32),
            pltpu.VMEM((8, length), F32),
            *[pltpu.VMEM((heads, length, size), F32)] * 3,
            *[pltpu.VMEM(tile, F32)] * 3,
            *[pltpu.VMEM((n_far, *tile), F32)] * 2,
            pltpu.VMEM((2, heads, size, size), F32),
            pltpu.VMEM((heads, size, size), F32),
            pltpu.VMEM((heads, size, size), BF16),
            pltpu.VMEM((n_far, heads, size, size), BF16),
            *[pltpu.VMEM((heads, size, size), F32)] * 2,
            pltpu.VMEM((2, heads, size, size), BF16),
            *[pltpu.VMEM((heads, length, size), F32)] * 3,
            pltpu.VMEM((3, heads, length, size), BF16),
            pltpu.VMEM((length, width), BF16),
            dma((5,)),
            dma((1,)),
            dma((1,)),
            dma((heads,)),
            dma((heads,)),
            dma((n_far,)),
            dma((n_far,)),
            dma((n_far, heads)),
            dma((n_far, heads)),
            dma((heads,)),
            dma((heads,)),
            dma((3, heads)),
            dma((3, heads)),
            dma((3,)),
        ],
        compiler_params=pltpu.CompilerParams(collective_id=0, has_side_effects=True),
    )(queries, keys, values, output_gradient, log_decay)


def solution(mesh):
    in_specs = (
        P("pipe", "seq", "head"),
        P("pipe", "seq", "head"),
        P("pipe", "seq", "head"),
        P("pipe", "seq", "head"),
        P("pipe", "head", "seq"),
    )
    out_specs = (P("pipe", "seq", "head"), P("pipe", "seq", "head"), P("pipe", "seq", "head"))
    body = functools.partial(per_device, mesh.shape["pipe"], mesh.shape["seq"])
    return jax.shard_map(body, mesh=mesh, in_specs=in_specs, out_specs=out_specs, check_vma=False)
```

time: 174 us -> 52 us (0.30)
  the two profiles are of different devices: /device:TPU:1 before, /device:TPU:48 now
where the time goes in v1:
time: 52 us; the launch traced here: 51.7 us
  Pallas kernels  47.6 us (92%)
  local copies, waits for them, and re-layouts  3.46 us (7%)
  between operations  0.65 us (1%)
    pallas_call x1, Pallas kernels, per_device(): pl.pallas_call(functools.partial(kernel, n_pipe, n_chip), out_shape=[jax....  47.6 us
    unnamed x7, local copies, waits for them, and re-layouts  3.46 us

profile of v1, /device:TPU:48, one launch (start us, length us, event | category | flops | bytes accessed | tf_op | source)
XLA Modules:
  0.0 51.7 jit_solution(16141389856557572965)
XLA Ops:
  0.6 47.6 %shard_map.76 = (bf16[1,256,512]{2,1,0:T(8,128)(2,1)}, bf16[1,256,512]{2,1,0:T(8,128)(2,1)}, bf16[1,256,512]{2,1,0:T(8,128)(2,1)}) custom-call(bf16[1,256,512]{2,1,0:T(8,128)(2,1)} %q_hbm.1, bf16[1,256,512]{2,1,0:T(8,128)(2,1)} %k_hbm.1, bf16[1,256,512]{2,1,0:T(8,128)(2,1)} %v_hbm.1, bf16[1,256,512]{2,1,0:T(8,128)(2,1)} %g_hbm.1, f32[1,4,256]{2,1,0:T(4,128)} %ld_hbm.1), custom_call_target="tpu_custom_call" | custom-call | tf_op jit(solution)/shard_map/pallas_call | solution.py:373
  48.3 0.0 copy-start.1
  48.3 1.7 %copy.11 = bf16[1,256,512]{2,1,0:T(8,128)(2,1)} copy(bf16[1,256,512]{2,1,0:T(8,128)(2,1)} %get-tuple-element.6) | data formatting | bytes 524288
  50.0 0.0 copy-done.1
  50.0 0.0 copy-start
  50.0 0.7 %copy.12 = bf16[1,256,512]{2,1,0:T(8,128)(2,1)} copy(bf16[1,256,512]{2,1,0:T(8,128)(2,1)S(1)} %copy-done.1) | data formatting | bytes 524288
  50.7 0.3 copy-done
  51.0 0.7 %copy.13 = bf16[1,256,512]{2,1,0:T(8,128)(2,1)} copy(bf16[1,256,512]{2,1,0:T(8,128)(2,1)S(1)} %copy-done) | data formatting | bytes 524288
Async XLA Ops:
  48.3 1.7 %copy-start.1 = (bf16[1,256,512]{2,1,0:T(8,128)(2,1)S(1)}, bf16[1,256,512]{2,1,0:T(8,128)(2,1)}, u32[]{:S(2)}) copy-start(bf16[1,256,512]{2,1,0:T(8,128)(2,1)} %get-tuple-element.7) | copy-start | bytes 786436
  50.0 1.0 %copy-start = (bf16[1,256,512]{2,1,0:T(8,128)(2,1)S(1)}, bf16[1,256,512]{2,1,0:T(8,128)(2,1)}, u32[]{:S(2)}) copy-start(bf16[1,256,512]{2,1,0:T(8,128)(2,1)} %get-tuple-element.8) | copy-start | bytes 786436

commit v2 on v1

v2 whole, which is shorter than its diff:
```python
import functools

import jax
import jax.numpy as jnp
from jax import lax
from jax.experimental import pallas as pl
from jax.experimental.pallas import tpu as pltpu
from jax.sharding import PartitionSpec as P

MESH = pl.DeviceIdType.MESH
INNER = (((1,), (1,)), ((), ()))
OUTER = (((0,), (0,)), ((), ()))
F32 = jnp.float32
BF16 = jnp.bfloat16


def mm(a, b):
    return jnp.dot(a, b, preferred_element_type=F32)


def mm_nt(a, b):
    return lax.dot_general(a, b, INNER, preferred_element_type=F32)


def mm_tn(a, b):
    return lax.dot_general(a, b, OUTER, preferred_element_type=F32)


def running_sums(ld, part_ref, cum_ref, tot_ref):
    heads, length = ld.shape
    high = ld.astype(BF16).astype(F32)
    rest = ld - high
    middle = rest.astype(BF16).astype(F32)
    part_ref[0:heads, :] = high
    part_ref[heads : 2 * heads, :] = middle
    part_ref[2 * heads : 3 * heads, :] = rest - middle
    earlier = (
        (
            lax.broadcasted_iota(jnp.int32, (length, length), 0)
            <= lax.broadcasted_iota(jnp.int32, (length, length), 1)
        )
        .astype(F32)
        .astype(BF16)
    )
    sums = mm(part_ref[...].astype(BF16), earlier)
    cum_ref[0:heads, :] = sums[0:heads] + sums[heads : 2 * heads] + sums[2 * heads : 3 * heads]
    tot_ref[...] = jnp.broadcast_to(cum_ref[:, length - 1 : length], tot_ref.shape)


def as_columns(cum_ref, h, half):
    blocks = []
    for b in range(2):
        row = cum_ref[h : h + 1, b * half : (b + 1) * half]
        blocks.append(jnp.broadcast_to(row, (half, half)).T)
    return jnp.concatenate(blocks, axis=0)


def kernel(
    n_pipe,
    n_chip,
    q_hbm,
    k_hbm,
    v_hbm,
    g_hbm,
    ld_hbm,
    oq_ref,
    ok_ref,
    ov_ref,
    q_ref,
    k_ref,
    v_ref,
    g_ref,
    ld_ref,
    part_ref,
    cum_ref,
    tot_ref,
    tot_sib_ref,
    chip_tot_ref,
    far_tot_ref,
    weight_ref,
    tail_ref,
    local_ref,
    sib_state_ref,
    agg_ref,
    far_ref,
    ship_ref,
    up_ref,
    up_ld_ref,
    up_state_ref,
    up_cum_ref,
    up_tot_ref,
    up_lead_ref,
    up_tail_ref,
    iq_ref,
    ik_ref,
    iv_ref,
    in_sem,
    tot_send,
    tot_recv,
    x_send,
    x_recv,
    ft_send,
    ft_recv,
    agg_send,
    agg_recv,
    ld_send,
    ld_recv,
    y_send,
    y_recv,
    st_send,
    st_recv,
    ready,
    low_ready,
    cross_ready,
):
    length, width = q_ref.shape
    heads = ld_ref.shape[1]
    size = width // heads
    half = length // 2
    n_far = n_chip - 1

    pipe = lax.axis_index("pipe")
    seq = lax.axis_index("seq")
    chip = lax.div(seq, 2)
    core = lax.rem(seq, 2)
    sibling = seq + 1 - 2 * core
    step = 2 * core - 1
    n_partner = core * (n_far - chip) + (1 - core) * chip
    below = lax.rem(pipe + n_pipe - 1, n_pipe)
    above = lax.rem(pipe + 1, n_pipe)
    is_source = pipe > 0
    is_target = pipe < n_pipe - 1

    def partner(d):
        return 2 * (chip + step * d) + (1 - core)

    def cols(ref, h):
        return ref[:, h * size : (h + 1) * size]

    def remote(src, dst, send, recv, device):
        return pltpu.make_async_remote_copy(
            src_ref=src,
            dst_ref=dst,
            send_sem=send,
            recv_sem=recv,
            device_id=device,
            device_id_type=MESH,
        )

    def signal(sem, device):
        pl.semaphore_signal(sem, inc=1, device_id=device, device_id_type=MESH)

    inputs = (q_hbm, g_hbm, k_hbm, v_hbm)
    held = (q_ref, g_ref, k_ref, v_ref)

    def tot_copy():
        return remote(tot_ref, tot_sib_ref, tot_send.at[0], tot_recv.at[0], {"seq": sibling})

    def x_copy(h):
        return remote(
            local_ref.at[core, h], sib_state_ref.at[h], x_send.at[h], x_recv.at[h], {"seq": sibling}
        )

    def tot_far(d):
        return remote(
            chip_tot_ref,
            far_tot_ref.at[d - 1],
            ft_send.at[d - 1],
            ft_recv.at[d - 1],
            {"seq": partner(d)},
        )

    def agg_far(d, h):
        return remote(
            agg_ref.at[h],
            far_ref.at[d - 1, h],
            agg_send.at[d - 1, h],
            agg_recv.at[d - 1, h],
            {"seq": partner(d)},
        )

    def ld_copy():
        return remote(ld_ref, up_ld_ref, ld_send.at[0], ld_recv.at[0], {"pipe": below})

    def y_copy(i, h):
        return remote(
            held[i].at[:, pl.ds(h * size, size)],
            up_ref.at[i, h],
            y_send.at[i, h],
            y_recv.at[i, h],
            {"pipe": below},
        )

    def st_copy(other, h):
        device = {"pipe": below, "seq": sibling if other else seq}
        return remote(
            ship_ref.at[other, h],
            up_state_ref.at[core, h],
            st_send.at[other, h],
            st_recv.at[core, h],
            device,
        )

    barrier = pltpu.get_barrier_semaphore()
    busy = jnp.minimum(pipe, 1)

    @pl.when(is_source)
    def _():
        signal(barrier, {"seq": sibling})

    @pl.when(pipe == 1)
    def _():
        signal(barrier, {"pipe": below})

    @pl.when(jnp.logical_and(is_source, is_target))
    def _():
        signal(barrier, {"pipe": above})

    loads = [pltpu.make_async_copy(ld_hbm, ld_ref, in_sem.at[4])]
    for i, (src, dst) in enumerate(zip(inputs, held)):
        loads.append(pltpu.make_async_copy(src.at[0], dst, in_sem.at[i]))
    @pl.when(is_source)
    def _():
        for load in loads:
            load.start()

    for d in range(1, n_far + 1):

        @pl.when(d > n_partner)
        def _():
            far_ref[d - 1] = jnp.zeros(far_ref.shape[1:], BF16)
            far_tot_ref[d - 1] = jnp.zeros(far_tot_ref.shape[1:], F32)

    part_ref[...] = jnp.zeros_like(part_ref)
    cum_ref[...] = jnp.zeros_like(cum_ref)
    up_cum_ref[...] = jnp.zeros_like(up_cum_ref)

    pl.semaphore_wait(barrier, 1 + busy * jnp.minimum(chip, 1) + jnp.minimum(lax.div(pipe, 2), 1))

    @pl.when(jnp.logical_and(is_source, chip < n_far))
    def _():
        signal(barrier, {"seq": seq + 2})

    @pl.when(pipe == 0)
    def _():
        signal(low_ready, {"pipe": above})

    @pl.when(pipe == 1)
    def _():
        pl.semaphore_wait(low_ready, 1)

    @pl.when(is_source)
    def _():
        signal(cross_ready, {"seq": sibling})
        for load in loads:
            load.wait()
        ld_copy().start()
        for h in range(heads):
            for i in range(4):
                y_copy(i, h).start()

    @pl.when(jnp.logical_and(is_source, core == 0))
    def _():
        for d in range(1, n_far + 1):

            @pl.when(d <= n_partner)
            def _():
                signal(ready.at[d - 1], {"seq": partner(d)})

    def make_aggregate(h):
        x_copy(h).wait_recv()
        agg_ref[h] = (
            jnp.exp(tot_ref[h : h + 1, :]) * sib_state_ref[h] + local_ref[1 - core, h]
        ).astype(BF16)

    @pl.when(is_source)
    def _():
        running_sums(ld_ref[0], part_ref, cum_ref, tot_ref)
        tot_copy().start()
        for h in range(heads):
            col = as_columns(cum_ref, h, half)
            lead = jnp.exp(col)
            tail_ref[h] = jnp.exp(tot_ref[h : h + 1, :] - col)
            query_weighted = (lead * cols(q_ref, h).astype(F32)).astype(BF16)
            local_ref[1, h] = mm_tn(query_weighted, cols(g_ref, h))

            @pl.when(core == 1)
            def _():
                x_copy(h).start()

        for h in range(heads):
            key_weighted = (tail_ref[h] * cols(k_ref, h).astype(F32)).astype(BF16)
            local_ref[0, h] = mm_tn(key_weighted, cols(v_ref, h))

            @pl.when(core == 0)
            def _():
                x_copy(h).start()

        tot_copy().wait_recv()
        chip_tot_ref[...] = tot_ref[...] + tot_sib_ref[...]

        @pl.when(core == 0)
        def _():
            for h in range(heads):
                make_aggregate(h)
            for i in range(n_far):

                @pl.when(i < n_partner)
                def _():
                    d = n_partner - i
                    tot_far(d).start()
                    for h in range(heads):
                        agg_far(d, h).start()

    at = lax.broadcasted_iota(jnp.int32, (half, half), 0)
    by = lax.broadcasted_iota(jnp.int32, (half, half), 1)
    lower, upper = at >= by, at <= by

    def inner_part(h):
        if h == 0:
            ld_copy().wait_recv()
            running_sums(up_ld_ref[0], part_ref, up_cum_ref, up_tot_ref)
        col = as_columns(up_cum_ref, h, half)
        up_lead_ref[h] = jnp.exp(col)
        up_tail_ref[h] = jnp.exp(up_tot_ref[h : h + 1, :] - col)
        for i in range(4):
            y_copy(i, h).wait_recv()
        q, g, k, v = (up_ref[i, h] for i in range(4))
        row0, row1 = up_cum_ref[h : h + 1, :half], up_cum_ref[h : h + 1, half:]
        col0, col1 = col[:half], col[half:]
        d00 = jnp.where(lower, jnp.exp(col0 - row0), 0.0)
        d10 = jnp.exp(col1 - row0)
        d11 = jnp.where(lower, jnp.exp(col1 - row1), 0.0)
        pair0 = (mm_nt(g[:half], v[:half]) * d00).astype(BF16)
        pair1 = (mm_nt(g[half:], v) * jnp.concatenate([d10, d11], axis=1)).astype(BF16)
        iq_ref[h, :half, :] = mm(pair0, k[:half])
        iq_ref[h, half:, :] = mm(pair1, k)
        e00 = jnp.where(upper, jnp.exp(row0 - col0), 0.0)
        e01 = jnp.exp(row1 - col0)
        e11 = jnp.where(upper, jnp.exp(row1 - col1), 0.0)
        e0 = jnp.concatenate([e00, e01], axis=1)
        pair_t0 = (mm_nt(v[:half], g) * e0).astype(BF16)
        pair_t1 = (mm_nt(v[half:], g[half:]) * e11).astype(BF16)
        ik_ref[h, :half, :] = mm(pair_t0, q)
        ik_ref[h, half:, :] = mm(pair_t1, q[half:])
        score_t0 = (mm_nt(k[:half], q) * e0).astype(BF16)
        score_t1 = (mm_nt(k[half:], q[half:]) * e11).astype(BF16)
        iv_ref[h, :half, :] = mm(score_t0, g)
        iv_ref[h, half:, :] = mm(score_t1, g[half:])

    def inner_parts(some):
        @pl.when(is_target)
        def _():
            for h in some:
                inner_part(h)

    inner_parts(range(heads // 2))

    @pl.when(jnp.logical_and(is_source, core == 1))
    def _():
        for h in range(heads):
            make_aggregate(h)
        for d in range(1, n_far + 1):

            @pl.when(d <= n_partner)
            def _():
                pl.semaphore_wait(ready.at[d - 1], 1)
                tot_far(d).start()
                for h in range(heads):
                    agg_far(d, h).start()

    inner_parts(range(heads // 2, heads - 1))

    @pl.when(is_source)
    def _():
        between = jnp.zeros(tot_ref.shape, F32)
        for d in range(1, n_far + 1):

            @pl.when(d <= n_partner)
            def _():
                tot_far(d).wait_recv()

            weight_ref[d - 1] = jnp.exp(between)
            between = between + far_tot_ref[d - 1]

        for h in range(heads):
            for d in range(1, n_far + 1):

                @pl.when(d <= n_partner)
                def _():
                    agg_far(d, h).wait_recv()

            total = jnp.zeros((size, size), F32)
            for d in range(1, n_far + 1):
                total = total + weight_ref[d - 1, h : h + 1, :] * far_ref[d - 1, h].astype(F32)
            ship_ref[0, h] = total.astype(BF16)
            ship_ref[1, h] = (
                jnp.exp(tot_ref[h : h + 1, :]) * total + local_ref[core, h]
            ).astype(BF16)
            if h == 0:
                pl.semaphore_wait(cross_ready, 1)
            st_copy(0, h).start()
            st_copy(1, h).start()

    inner_parts(range(heads - 1, heads))

    @pl.when(is_target)
    def _():
        for h in range(heads):
            here = slice(h * size, (h + 1) * size)
            g, k, v = (up_ref[i, h] for i in (1, 2, 3))
            for i in range(2):
                remote(
                    ship_ref.at[0, h],
                    up_state_ref.at[i, h],
                    st_send.at[0, h],
                    st_recv.at[i, h],
                    {"pipe": below},
                ).wait_recv()
            state_in, state_rev = up_state_ref[0, h], up_state_ref[1, h]
            lead, tail = up_lead_ref[h], up_tail_ref[h]
            oq_ref[0, :, here] = (iq_ref[h] + lead * mm_nt(g, state_in)).astype(BF16)
            ok_ref[0, :, here] = (ik_ref[h] + tail * mm_nt(v, state_rev)).astype(BF16)
            ov_ref[0, :, here] = (iv_ref[h] + tail * mm(k, state_rev)).astype(BF16)

    @pl.when(jnp.logical_not(is_target))
    def _():
        for o in (oq_ref, ok_ref, ov_ref):
            o[...] = jnp.zeros_like(o)

    @pl.when(is_source)
    def _():
        tot_copy().wait_send()
        for h in range(heads):
            x_copy(h).wait_send()
        for d in range(1, n_far + 1):

            @pl.when(d <= n_partner)
            def _():
                tot_far(d).wait_send()
                for h in range(heads):
                    agg_far(d, h).wait_send()

        ld_copy().wait_send()
        for h in range(heads):
            for i in range(4):
                y_copy(i, h).wait_send()
            for i in range(2):
                st_copy(i, h).wait_send()


def put_kernel(a_ref, b_ref, c_ref, oa_ref, ob_ref, oc_ref, sem):
    copies = [
        pltpu.make_async_copy(src, dst, sem.at[i])
        for i, (src, dst) in enumerate(((a_ref, oa_ref), (b_ref, ob_ref), (c_ref, oc_ref)))
    ]
    for copy in copies:
        copy.start()
    for copy in copies:
        copy.wait()


def per_device(n_pipe, n_seq, queries, keys, values, output_gradient, log_decay):
    length, width = queries.shape[1:]
    heads = log_decay.shape[1]
    size = width // heads
    n_chip = n_seq // 2
    n_far = n_chip - 1
    dma = pltpu.SemaphoreType.DMA
    tile = (8, size)
    anywhere = pl.BlockSpec(memory_space=pl.ANY)
    vmem = pl.BlockSpec(memory_space=pltpu.VMEM)
    shapes = [jax.ShapeDtypeStruct(queries.shape, BF16)] * 3
    results = pl.pallas_call(
        functools.partial(kernel, n_pipe, n_chip),
        out_shape=shapes,
        in_specs=[pl.BlockSpec(memory_space=pltpu.HBM)] * 5,
        out_specs=[vmem] * 3,
        scratch_shapes=[
            *[pltpu.VMEM((length, width), BF16)] * 4,
            pltpu.VMEM((1, heads, length), F32),
            pltpu.VMEM((16, length), F32),
            pltpu.VMEM((8, length), F32),
            *[pltpu.VMEM(tile, F32)] * 3,
            *[pltpu.VMEM((n_far, *tile), F32)] * 2,
            pltpu.VMEM((heads, length, size), F32),
            pltpu.VMEM((2, heads, size, size), F32),
            pltpu.VMEM((heads, size, size), F32),
            pltpu.VMEM((heads, size, size), BF16),
            pltpu.VMEM((n_far, heads, size, size), BF16),
            pltpu.VMEM((2, heads, size, size), BF16),
            pltpu.VMEM((4, heads, length, size), BF16),
            pltpu.VMEM((1, heads, length), F32),
            pltpu.VMEM((2, heads, size, size), BF16),
            pltpu.VMEM((8, length), F32),
            pltpu.VMEM(tile, F32),
            *[pltpu.VMEM((heads, length, size), F32)] * 5,
            dma((5,)),
            dma((1,)),
            dma((1,)),
            dma((heads,)),
            dma((heads,)),
            dma((n_far,)),
            dma((n_far,)),
            dma((n_far, heads)),
            dma((n_far, heads)),
            dma((1,)),
            dma((1,)),
            dma((4, heads)),
            dma((4, heads)),
            dma((2, heads)),
            dma((2, heads)),
            pltpu.SemaphoreType.REGULAR((n_far,)),
            pltpu.SemaphoreType.REGULAR,
            pltpu.SemaphoreType.REGULAR,
        ],
        compiler_params=pltpu.CompilerParams(
            collective_id=0, has_side_effects=True, vmem_limit_bytes=24 << 20
        ),
    )(
        *(
            pltpu.with_memory_space_constraint(x, pltpu.HBM)
            for x in (queries, keys, values, output_gradient, log_decay)
        )
    )
    return pl.pallas_call(
        put_kernel,
        out_shape=shapes,
        in_specs=[anywhere] * 3,
        out_specs=[anywhere] * 3,
        scratch_shapes=[dma((3,))],
        compiler_params=pltpu.CompilerParams(vmem_limit_bytes=4 << 20),
    )(*results)


def solution(mesh):
    in_specs = (
        P("pipe", "seq", "head"),
        P("pipe", "seq", "head"),
        P("pipe", "seq", "head"),
        P("pipe", "seq", "head"),
        P("pipe", "head", "seq"),
    )
    out_specs = (P("pipe", "seq", "head"), P("pipe", "seq", "head"), P("pipe", "seq", "head"))
    body = functools.partial(per_device, mesh.shape["pipe"], mesh.shape["seq"])
    return jax.shard_map(body, mesh=mesh, in_specs=in_specs, out_specs=out_specs, check_vma=False)
```

time: 52 us -> 37.7 us (0.73)
  the two profiles are of different devices: /device:TPU:48 before, /device:TPU:1 now
where the time goes in v2:
time: 37.7 us; the launch traced here: 37.6 us
  Pallas kernels  37 us (98%)
  between operations  0.64 us (2%)
    pallas_call x1, Pallas kernels, per_device(): pl.pallas_call(functools.partial(kernel, n_pipe, n_chip), out_shape=shape...  36 us
    pallas_call x1, Pallas kernels, per_device(): pl.pallas_call(put_kernel, out_shape=shapes, in_specs=[anywhere] * 3, out...  0.9 us

profile of v2, /device:TPU:1, one launch (start us, length us, event | category | flops | bytes accessed | tf_op | source)
XLA Modules:
  0.0 37.6 jit_solution(8871490904041310098)
XLA Ops:
  0.6 36.0 %shard_map.76 = (bf16[1,256,512]{2,1,0:T(8,128)(2,1)S(1)}, bf16[1,256,512]{2,1,0:T(8,128)(2,1)S(1)}, bf16[1,256,512]{2,1,0:T(8,128)(2,1)S(1)}) custom-call(bf16[1,256,512]{2,1,0:T(8,128)(2,1)} %q_hbm.1, bf16[1,256,512]{2,1,0:T(8,128)(2,1)} %k_hbm.1, bf16[1,256,512]{2,1,0:T(8,128)(2,1)} %v_hbm.1, bf16[1,256,512]{2,1,0:T(8,128)(2,1)} %g_hbm.1, f32[1,4,256]{2,1,0:T(4,128)} %ld_hbm.1), custom_call_target="tpu_custom_call" | custom-call | tf_op jit(solution)/shard_map/pallas_call | solution.py:474
  36.7 0.9 %shard_map.77 = (bf16[1,256,512]{2,1,0:T(8,128)(2,1)}, bf16[1,256,512]{2,1,0:T(8,128)(2,1)}, bf16[1,256,512]{2,1,0:T(8,128)(2,1)}) custom-call(bf16[1,256,512]{2,1,0:T(8,128)(2,1)S(1)} %get-tuple-element.6.a_ref, bf16[1,256,512]{2,1,0:T(8,128)(2,1)S(1)} %get-tuple-element.7.b_ref, bf16[1,256,512]{2,1,0:T(8,128)(2,1)S(1)} %get-tuple-element.8.c_ref), custom_call_target="tpu_custom_call" | custom-call | tf_op jit(solution)/shard_map/pallas_call | solution.py:526

commit v3 on v2

--- a/solution.py
+++ b/solution.py
@@ -87,8 +87,12 @@
     up_ref,
     up_ld_ref,
     up_state_ref,
+    up_sib_state_ref,
+    up_local_ref,
+    up_sib_local_ref,
     up_cum_ref,
     up_tot_ref,
+    up_tot_sib_ref,
     up_lead_ref,
     up_tail_ref,
     iq_ref,
@@ -109,9 +113,16 @@
     y_recv,
     st_send,
     st_recv,
+    et_send,
+    et_recv,
+    ex_send,
+    ex_recv,
+    eu_send,
+    eu_recv,
     ready,
     low_ready,
     cross_ready,
+    sib_ready,
 ):
     length, width = q_ref.shape
     heads = ld_ref.shape[1]
@@ -191,14 +202,30 @@
             {"pipe": below},
         )
 
-    def st_copy(other, h):
-        device = {"pipe": below, "seq": sibling if other else seq}
+    def st_copy(h):
         return remote(
-            ship_ref.at[other, h],
+            ship_ref.at[h],
             up_state_ref.at[core, h],
-            st_send.at[other, h],
-            st_recv.at[core, h],
-            device,
+            st_send.at[h],
+            st_recv.at[h],
+            {"pipe": below},
+        )
+
+    def up_tot_copy():
+        return remote(up_tot_ref, up_tot_sib_ref, et_send.at[0], et_recv.at[0], {"seq": sibling})
+
+    def up_local_copy(h):
+        return remote(
+            up_local_ref.at[h], up_sib_local_ref.at[h], ex_send.at[h], ex_recv.at[h], {"seq": sibling}
+        )
+
+    def up_state_copy(h):
+        return remote(
+            up_state_ref.at[core, h],
+            up_sib_state_ref.at[h],
+            eu_send.at[h],
+            eu_recv.at[h],
+            {"seq": sibling},
         )
 
     barrier = pltpu.get_barrier_semaphore()
@@ -224,6 +251,38 @@
         for load in loads:
             load.start()
 
+    pl.semaphore_wait(barrier, 1 + busy * jnp.minimum(chip, 1) + jnp.minimum(lax.div(pipe, 2), 1))
+
+    @pl.when(jnp.logical_and(is_source, chip < n_far))
+    def _():
+        signal(barrier, {"seq": seq + 2})
+
+    @pl.when(pipe == 0)
+    def _():
+        signal(low_ready, {"pipe": above})
+
+    @pl.when(pipe == 1)
+    def _():
+        pl.semaphore_wait(low_ready, 1)
+        signal(cross_ready, {"seq": sibling})
+
+    @pl.when(is_source)
+    def _():
+        for load in loads:
+            load.wait()
+        ld_copy().start()
+        for h in range(heads):
+            for i in range(4):
+                y_copy(i, h).start()
+
+    @pl.when(jnp.logical_and(is_source, core == 0))
+    def _():
+        for d in range(1, n_far + 1):
+
+            @pl.when(d <= n_partner)
+            def _():
+                signal(ready.at[d - 1], {"seq": partner(d)})
+
     for d in range(1, n_far + 1):
 
         @pl.when(d > n_partner)
@@ -234,38 +293,6 @@
     part_ref[...] = jnp.zeros_like(part_ref)
     cum_ref[...] = jnp.zeros_like(cum_ref)
     up_cum_ref[...] = jnp.zeros_like(up_cum_ref)
-
-    pl.semaphore_wait(barrier, 1 + busy * jnp.minimum(chip, 1) + jnp.minimum(lax.div(pipe, 2), 1))
-
-    @pl.when(jnp.logical_and(is_source, chip < n_far))
-    def _():
-        signal(barrier, {"seq": seq + 2})
-
-    @pl.when(pipe == 0)
-    def _():
-        signal(low_ready, {"pipe": above})
-
-    @pl.when(pipe == 1)
-    def _():
-        pl.semaphore_wait(low_ready, 1)
-
-    @pl.when(is_source)
-    def _():
-        signal(cross_ready, {"seq": sibling})
-        for load in loads:
-            load.wait()
-        ld_copy().start()
-        for h in range(heads):
-            for i in range(4):
-                y_copy(i, h).start()
-
-    @pl.when(jnp.logical_and(is_source, core == 0))
-    def _():
-        for d in range(1, n_far + 1):
-
-            @pl.when(d <= n_partner)
-            def _():
-                signal(ready.at[d - 1], {"seq": partner(d)})
 
     def make_aggregate(h):
         x_copy(h).wait_recv()
@@ -348,13 +375,36 @@
         iv_ref[h, :half, :] = mm(score_t0, g)
         iv_ref[h, half:, :] = mm(score_t1, g[half:])
 
+        @pl.when(core == 0)
+        def _():
+            key_weighted = (up_tail_ref[h] * k.astype(F32)).astype(BF16)
+            up_local_ref[h] = mm_tn(key_weighted, v)
+
+        @pl.when(core == 1)
+        def _():
+            query_weighted = (up_lead_ref[h] * q.astype(F32)).astype(BF16)
+            up_local_ref[h] = mm_tn(query_weighted, g)
+
     def inner_parts(some):
         @pl.when(is_target)
         def _():
             for h in some:
                 inner_part(h)
 
+    def exchange(some):
+        @pl.when(is_target)
+        def _():
+            for h in some:
+                if h == 0:
+                    up_tot_copy().start()
+                up_local_copy(h).start()
+
     inner_parts(range(heads // 2))
+
+    @pl.when(pipe == 1)
+    def _():
+        pl.semaphore_wait(cross_ready, 1)
+        signal(sib_ready, {"pipe": below})
 
     @pl.when(jnp.logical_and(is_source, core == 1))
     def _():
@@ -371,6 +421,12 @@
 
     inner_parts(range(heads // 2, heads - 1))
 
+    @pl.when(pipe == 0)
+    def _():
+        pl.semaphore_wait(sib_ready, 1)
+
+    exchange(range(heads - 1))
+
     @pl.when(is_source)
     def _():
         between = jnp.zeros(tot_ref.shape, F32)
@@ -393,30 +449,27 @@
             total = jnp.zeros((size, size), F32)
             for d in range(1, n_far + 1):
                 total = total + weight_ref[d - 1, h : h + 1, :] * far_ref[d - 1, h].astype(F32)
-            ship_ref[0, h] = total.astype(BF16)
-            ship_ref[1, h] = (
-                jnp.exp(tot_ref[h : h + 1, :]) * total + local_ref[core, h]
-            ).astype(BF16)
-            if h == 0:
-                pl.semaphore_wait(cross_ready, 1)
-            st_copy(0, h).start()
-            st_copy(1, h).start()
+            ship_ref[h] = total.astype(BF16)
+            st_copy(h).start()
 
     inner_parts(range(heads - 1, heads))
+    exchange(range(heads - 1, heads))
 
     @pl.when(is_target)
     def _():
+        for h in range(heads):
+            st_copy(h).wait_recv()
+            up_state_copy(h).start()
+        up_tot_copy().wait_recv()
         for h in range(heads):
             here = slice(h * size, (h + 1) * size)
             g, k, v = (up_ref[i, h] for i in (1, 2, 3))
-            for i in range(2):
-                remote(
-                    ship_ref.at[0, h],
-                    up_state_ref.at[i, h],
-                    st_send.at[0, h],
-                    st_recv.at[i, h],
-                    {"pipe": below},
-                ).wait_recv()
+            up_local_copy(h).wait_recv()
+            up_state_copy(h).wait_recv()
+            up_state_ref[1 - core, h] = (
+                jnp.exp(up_tot_sib_ref[h : h + 1, :]) * up_sib_state_ref[h].astype(F32)
+                + up_sib_local_ref[h]
+            ).astype(BF16)
             state_in, state_rev = up_state_ref[0, h], up_state_ref[1, h]
             lead, tail = up_lead_ref[h], up_tail_ref[h]
             oq_ref[0, :, here] = (iq_ref[h] + lead * mm_nt(g, state_in)).astype(BF16)
@@ -445,8 +498,14 @@
         for h in range(heads):
             for i in range(4):
                 y_copy(i, h).wait_send()
-            for i in range(2):
-                st_copy(i, h).wait_send()
+            st_copy(h).wait_send()
+
+    @pl.when(is_target)
+    def _():
+        up_tot_copy().wait_send()
+        for h in range(heads):
+            up_local_copy(h).wait_send()
+            up_state_copy(h).wait_send()
 
 
 def put_kernel(a_ref, b_ref, c_ref, oa_ref, ob_ref, oc_ref, sem):
@@ -488,12 +547,14 @@
             pltpu.VMEM((heads, size, size), F32),
             pltpu.VMEM((heads, size, size), BF16),
             pltpu.VMEM((n_far, heads, size, size), BF16),
-            pltpu.VMEM((2, heads, size, size), BF16),
+            pltpu.VMEM((heads, size, size), BF16),
             pltpu.VMEM((4, heads, length, size), BF16),
             pltpu.VMEM((1, heads, length), F32),
             pltpu.VMEM((2, heads, size, size), BF16),
+            pltpu.VMEM((heads, size, size), BF16),
+            *[pltpu.VMEM((heads, size, size), F32)] * 2,
             pltpu.VMEM((8, length), F32),
-            pltpu.VMEM(tile, F32),
+            *[pltpu.VMEM(tile, F32)] * 2,
             *[pltpu.VMEM((heads, length, size), F32)] * 5,
             dma((5,)),
             dma((1,)),
@@ -508,11 +569,13 @@
             dma((1,)),
             dma((4, heads)),
             dma((4, heads)),
-            dma((2, heads)),
-            dma((2, heads)),
+            dma((heads,)),
+            dma((heads,)),
+            dma((1,)),
+            dma((1,)),
+            *[dma((heads,))] * 4,
             pltpu.SemaphoreType.REGULAR((n_far,)),
-            pltpu.SemaphoreType.REGULAR,
-            pltpu.SemaphoreType.REGULAR,
+            *[pltpu.SemaphoreType.REGULAR] * 3,
         ],
         compiler_params=pltpu.CompilerParams(
             collective_id=0, has_side_effects=True, vmem_limit_bytes=24 << 20

time: 37.7 us -> 36.1 us (0.958)
  Pallas kernels: 37 us -> 35.4 us
    pallas_call x1, Pallas kernels: 36 us -> 34.5 us  [per_device(): pl.pallas_call(functools.partial(kernel, n_pipe, n_chip), out_shape=shape...]
where the time goes in v3:
time: 36.1 us; the launch traced here: 36 us
  Pallas kernels  35.4 us (98%)
  between operations  0.64 us (2%)
    pallas_call x1, Pallas kernels, per_device(): pl.pallas_call(functools.partial(kernel, n_pipe, n_chip), out_shape=shape...  34.5 us
    pallas_call x1, Pallas kernels, per_device(): pl.pallas_call(put_kernel, out_shape=shapes, in_specs=[anywhere] * 3, out...  0.9 us

profile of v3, /device:TPU:1, one launch (start us, length us, event | category | flops | bytes accessed | tf_op | source)
XLA Modules:
  0.0 36.0 jit_solution(16886646959878943953)
XLA Ops:
  0.6 34.5 %shard_map.76 = (bf16[1,256,512]{2,1,0:T(8,128)(2,1)S(1)}, bf16[1,256,512]{2,1,0:T(8,128)(2,1)S(1)}, bf16[1,256,512]{2,1,0:T(8,128)(2,1)S(1)}) custom-call(bf16[1,256,512]{2,1,0:T(8,128)(2,1)} %q_hbm.1, bf16[1,256,512]{2,1,0:T(8,128)(2,1)} %k_hbm.1, bf16[1,256,512]{2,1,0:T(8,128)(2,1)} %v_hbm.1, bf16[1,256,512]{2,1,0:T(8,128)(2,1)} %g_hbm.1, f32[1,4,256]{2,1,0:T(4,128)} %ld_hbm.1), custom_call_target="tpu_custom_call" | custom-call | tf_op jit(solution)/shard_map/pallas_call | solution.py:533
  35.1 0.9 %shard_map.77 = (bf16[1,256,512]{2,1,0:T(8,128)(2,1)}, bf16[1,256,512]{2,1,0:T(8,128)(2,1)}, bf16[1,256,512]{2,1,0:T(8,128)(2,1)}) custom-call(bf16[1,256,512]{2,1,0:T(8,128)(2,1)S(1)} %get-tuple-element.6.a_ref, bf16[1,256,512]{2,1,0:T(8,128)(2,1)S(1)} %get-tuple-element.7.b_ref, bf16[1,256,512]{2,1,0:T(8,128)(2,1)S(1)} %get-tuple-element.8.c_ref), custom_call_target="tpu_custom_call" | custom-call | tf_op jit(solution)/shard_map/pallas_call | solution.py:589

commit v4 on v3

--- a/solution.py
+++ b/solution.py
@@ -55,9 +55,14 @@
     return jnp.concatenate(blocks, axis=0)
 
 
+def weighted_state(x, weights, y):
+    return mm((x.T.astype(F32) * weights).astype(BF16), y)
+
+
 def kernel(
     n_pipe,
     n_chip,
+    n_late,
     q_hbm,
     k_hbm,
     v_hbm,
@@ -78,7 +83,6 @@
     chip_tot_ref,
     far_tot_ref,
     weight_ref,
-    tail_ref,
     local_ref,
     sib_state_ref,
     agg_ref,
@@ -141,6 +145,7 @@
     above = lax.rem(pipe + 1, n_pipe)
     is_source = pipe > 0
     is_target = pipe < n_pipe - 1
+    late_states = chip < n_late
 
     def partner(d):
         return 2 * (chip + step * d) + (1 - core)
@@ -167,9 +172,9 @@
     def tot_copy():
         return remote(tot_ref, tot_sib_ref, tot_send.at[0], tot_recv.at[0], {"seq": sibling})
 
-    def x_copy(h):
+    def x_copy():
         return remote(
-            local_ref.at[core, h], sib_state_ref.at[h], x_send.at[h], x_recv.at[h], {"seq": sibling}
+            local_ref.at[core], sib_state_ref, x_send.at[0], x_recv.at[0], {"seq": sibling}
         )
 
     def tot_far(d):
@@ -181,12 +186,12 @@
             {"seq": partner(d)},
         )
 
-    def agg_far(d, h):
+    def agg_far(d):
         return remote(
-            agg_ref.at[h],
-            far_ref.at[d - 1, h],
-            agg_send.at[d - 1, h],
-            agg_recv.at[d - 1, h],
+            agg_ref,
+            far_ref.at[d - 1],
+            agg_send.at[d - 1],
+            agg_recv.at[d - 1],
             {"seq": partner(d)},
         )
 
@@ -228,6 +233,15 @@
             {"seq": sibling},
         )
 
+    def ship(some):
+        for which, order in ((0, (2, 3, 0, 1)), (1, (0, 1, 2, 3))):
+
+            @pl.when(core == which)
+            def _():
+                for h in some:
+                    for i in order:
+                        y_copy(i, h).start()
+
     barrier = pltpu.get_barrier_semaphore()
     busy = jnp.minimum(pipe, 1)
 
@@ -271,9 +285,13 @@
         for load in loads:
             load.wait()
         ld_copy().start()
-        for h in range(heads):
-            for i in range(4):
-                y_copy(i, h).start()
+        ship(range(heads - 1))
+
+    last_first = jnp.logical_and(late_states, core == 1)
+
+    @pl.when(jnp.logical_and(is_source, last_first))
+    def _():
+        ship(range(heads - 1, heads))
 
     @pl.when(jnp.logical_and(is_source, core == 0))
     def _():
@@ -282,6 +300,51 @@
             @pl.when(d <= n_partner)
             def _():
                 signal(ready.at[d - 1], {"seq": partner(d)})
+
+    part_ref[...] = jnp.zeros_like(part_ref)
+    cum_ref[...] = jnp.zeros_like(cum_ref)
+    up_cum_ref[...] = jnp.zeros_like(up_cum_ref)
+
+    def make_aggregates():
+        x_copy().wait_recv()
+        for h in range(heads):
+            agg_ref[h] = (
+                jnp.exp(tot_ref[h : h + 1, :]) * sib_state_ref[h] + local_ref[1 - core, h]
+            ).astype(BF16)
+
+    @pl.when(is_source)
+    def _():
+        running_sums(ld_ref[0], part_ref, cum_ref, tot_ref)
+        tot_copy().start()
+        lead = jnp.exp(cum_ref[...])
+        tail = jnp.exp(tot_ref[:, :1] - cum_ref[...])
+        for h in range(heads):
+            local_ref[1, h] = weighted_state(cols(q_ref, h), lead[h : h + 1, :], cols(g_ref, h))
+
+        @pl.when(core == 1)
+        def _():
+            x_copy().start()
+
+        for h in range(heads):
+            local_ref[0, h] = weighted_state(cols(k_ref, h), tail[h : h + 1, :], cols(v_ref, h))
+
+        @pl.when(core == 0)
+        def _():
+            x_copy().start()
+
+        tot_copy().wait_recv()
+        chip_tot_ref[...] = tot_ref[...] + tot_sib_ref[...]
+
+        @pl.when(core == 0)
+        def _():
+            make_aggregates()
+            for i in range(n_far):
+
+                @pl.when(i < n_partner)
+                def _():
+                    d = n_partner - i
+                    tot_far(d).start()
+                    agg_far(d).start()
 
     for d in range(1, n_far + 1):
 
@@ -290,68 +353,40 @@
             far_ref[d - 1] = jnp.zeros(far_ref.shape[1:], BF16)
             far_tot_ref[d - 1] = jnp.zeros(far_tot_ref.shape[1:], F32)
 
-    part_ref[...] = jnp.zeros_like(part_ref)
-    cum_ref[...] = jnp.zeros_like(cum_ref)
-    up_cum_ref[...] = jnp.zeros_like(up_cum_ref)
-
-    def make_aggregate(h):
-        x_copy(h).wait_recv()
-        agg_ref[h] = (
-            jnp.exp(tot_ref[h : h + 1, :]) * sib_state_ref[h] + local_ref[1 - core, h]
-        ).astype(BF16)
-
-    @pl.when(is_source)
-    def _():
-        running_sums(ld_ref[0], part_ref, cum_ref, tot_ref)
-        tot_copy().start()
-        for h in range(heads):
-            col = as_columns(cum_ref, h, half)
-            lead = jnp.exp(col)
-            tail_ref[h] = jnp.exp(tot_ref[h : h + 1, :] - col)
-            query_weighted = (lead * cols(q_ref, h).astype(F32)).astype(BF16)
-            local_ref[1, h] = mm_tn(query_weighted, cols(g_ref, h))
-
-            @pl.when(core == 1)
-            def _():
-                x_copy(h).start()
-
-        for h in range(heads):
-            key_weighted = (tail_ref[h] * cols(k_ref, h).astype(F32)).astype(BF16)
-            local_ref[0, h] = mm_tn(key_weighted, cols(v_ref, h))
-
-            @pl.when(core == 0)
-            def _():
-                x_copy(h).start()
-
-        tot_copy().wait_recv()
-        chip_tot_ref[...] = tot_ref[...] + tot_sib_ref[...]
-
-        @pl.when(core == 0)
-        def _():
-            for h in range(heads):
-                make_aggregate(h)
-            for i in range(n_far):
-
-                @pl.when(i < n_partner)
-                def _():
-                    d = n_partner - i
-                    tot_far(d).start()
-                    for h in range(heads):
-                        agg_far(d, h).start()
-
     at = lax.broadcasted_iota(jnp.int32, (half, half), 0)
     by = lax.broadcasted_iota(jnp.int32, (half, half), 1)
     lower, upper = at >= by, at <= by
 
-    def inner_part(h):
+    def sibling_part(h):
         if h == 0:
             ld_copy().wait_recv()
             running_sums(up_ld_ref[0], part_ref, up_cum_ref, up_tot_ref)
+        row = up_cum_ref[h : h + 1, :]
+
+        @pl.when(core == 0)
+        def _():
+            y_copy(2, h).wait_recv()
+            y_copy(3, h).wait_recv()
+            weights = jnp.exp(up_tot_ref[h : h + 1, :1] - row)
+            up_local_ref[h] = weighted_state(up_ref[2, h], weights, up_ref[3, h])
+
+        @pl.when(core == 1)
+        def _():
+            y_copy(0, h).wait_recv()
+            y_copy(1, h).wait_recv()
+            up_local_ref[h] = weighted_state(up_ref[0, h], jnp.exp(row), up_ref[1, h])
+
+    def inner_part(h):
         col = as_columns(up_cum_ref, h, half)
         up_lead_ref[h] = jnp.exp(col)
         up_tail_ref[h] = jnp.exp(up_tot_ref[h : h + 1, :] - col)
-        for i in range(4):
-            y_copy(i, h).wait_recv()
+        for which, rest in ((0, (0, 1)), (1, (2, 3))):
+
+            @pl.when(core == which)
+            def _():
+                for i in rest:
+                    y_copy(i, h).wait_recv()
+
         q, g, k, v = (up_ref[i, h] for i in range(4))
         row0, row1 = up_cum_ref[h : h + 1, :half], up_cum_ref[h : h + 1, half:]
         col0, col1 = col[:half], col[half:]
@@ -375,57 +410,69 @@
         iv_ref[h, :half, :] = mm(score_t0, g)
         iv_ref[h, half:, :] = mm(score_t1, g[half:])
 
-        @pl.when(core == 0)
-        def _():
-            key_weighted = (up_tail_ref[h] * k.astype(F32)).astype(BF16)
-            up_local_ref[h] = mm_tn(key_weighted, v)
-
-        @pl.when(core == 1)
-        def _():
-            query_weighted = (up_lead_ref[h] * q.astype(F32)).astype(BF16)
-            up_local_ref[h] = mm_tn(query_weighted, g)
-
-    def inner_parts(some):
-        @pl.when(is_target)
-        def _():
-            for h in some:
-                inner_part(h)
-
-    def exchange(some):
-        @pl.when(is_target)
-        def _():
-            for h in some:
-                if h == 0:
-                    up_tot_copy().start()
-                up_local_copy(h).start()
-
-    inner_parts(range(heads // 2))
-
-    @pl.when(pipe == 1)
-    def _():
-        pl.semaphore_wait(cross_ready, 1)
-        signal(sib_ready, {"pipe": below})
+    def result(h):
+        here = slice(h * size, (h + 1) * size)
+        g, k, v = (up_ref[i, h] for i in (1, 2, 3))
+        up_local_copy(h).wait_recv()
+        up_state_copy(h).wait_recv()
+        up_state_ref[1 - core, h] = (
+            jnp.exp(up_tot_sib_ref[h : h + 1, :]) * up_sib_state_ref[h].astype(F32)
+            + up_sib_local_ref[h]
+        ).astype(BF16)
+        state_in, state_rev = up_state_ref[0, h], up_state_ref[1, h]
+        for b in range(2):
+            rows = slice(b * half, (b + 1) * half)
+            lead, tail = up_lead_ref[h, rows, :], up_tail_ref[h, rows, :]
+            oq_ref[0, rows, here] = (
+                iq_ref[h, rows, :] + lead * mm_nt(g[rows], state_in)
+            ).astype(BF16)
+            ok_ref[0, rows, here] = (
+                ik_ref[h, rows, :] + tail * mm_nt(v[rows], state_rev)
+            ).astype(BF16)
+            ov_ref[0, rows, here] = (iv_ref[h, rows, :] + tail * mm(k[rows], state_rev)).astype(
+                BF16
+            )
+
+    half_heads = heads // 2
 
     @pl.when(jnp.logical_and(is_source, core == 1))
     def _():
-        for h in range(heads):
-            make_aggregate(h)
+        make_aggregates()
         for d in range(1, n_far + 1):
 
             @pl.when(d <= n_partner)
             def _():
                 pl.semaphore_wait(ready.at[d - 1], 1)
                 tot_far(d).start()
-                for h in range(heads):
-                    agg_far(d, h).start()
-
-    inner_parts(range(heads // 2, heads - 1))
+                agg_far(d).start()
+
+    @pl.when(is_target)
+    def _():
+        for h in range(half_heads):
+            sibling_part(h)
+            inner_part(h)
+
+    @pl.when(pipe == 1)
+    def _():
+        pl.semaphore_wait(cross_ready, 1)
+        signal(sib_ready, {"pipe": below})
+
+    def middle_heads():
+        up_tot_copy().start()
+        for h in range(half_heads):
+            up_local_copy(h).start()
+        for h in range(half_heads, heads - 1):
+            sibling_part(h)
+            up_local_copy(h).start()
+            inner_part(h)
 
     @pl.when(pipe == 0)
     def _():
         pl.semaphore_wait(sib_ready, 1)
 
-    exchange(range(heads - 1))
+    @pl.when(jnp.logical_and(is_target, last_first))
+    def _():
+        middle_heads()
 
     @pl.when(is_source)
     def _():
@@ -435,25 +482,31 @@
             @pl.when(d <= n_partner)
             def _():
                 tot_far(d).wait_recv()
+                agg_far(d).wait_recv()
 
             weight_ref[d - 1] = jnp.exp(between)
             between = between + far_tot_ref[d - 1]
 
         for h in range(heads):
-            for d in range(1, n_far + 1):
-
-                @pl.when(d <= n_partner)
-                def _():
-                    agg_far(d, h).wait_recv()
-
             total = jnp.zeros((size, size), F32)
             for d in range(1, n_far + 1):
                 total = total + weight_ref[d - 1, h : h + 1, :] * far_ref[d - 1, h].astype(F32)
             ship_ref[h] = total.astype(BF16)
             st_copy(h).start()
 
-    inner_parts(range(heads - 1, heads))
-    exchange(range(heads - 1, heads))
+    @pl.when(jnp.logical_and(is_source, jnp.logical_not(last_first)))
+    def _():
+        ship(range(heads - 1, heads))
+
+    @pl.when(jnp.logical_and(is_target, jnp.logical_not(last_first)))
+    def _():
+        middle_heads()
+
+    @pl.when(jnp.logical_and(is_target, last_first))
+    def _():
+        sibling_part(heads - 1)
+        up_local_copy(heads - 1).start()
+        inner_part(heads - 1)
 
     @pl.when(is_target)
     def _():
@@ -461,38 +514,31 @@
             st_copy(h).wait_recv()
             up_state_copy(h).start()
         up_tot_copy().wait_recv()
-        for h in range(heads):
-            here = slice(h * size, (h + 1) * size)
-            g, k, v = (up_ref[i, h] for i in (1, 2, 3))
-            up_local_copy(h).wait_recv()
-            up_state_copy(h).wait_recv()
-            up_state_ref[1 - core, h] = (
-                jnp.exp(up_tot_sib_ref[h : h + 1, :]) * up_sib_state_ref[h].astype(F32)
-                + up_sib_local_ref[h]
-            ).astype(BF16)
-            state_in, state_rev = up_state_ref[0, h], up_state_ref[1, h]
-            lead, tail = up_lead_ref[h], up_tail_ref[h]
-            oq_ref[0, :, here] = (iq_ref[h] + lead * mm_nt(g, state_in)).astype(BF16)
-            ok_ref[0, :, here] = (ik_ref[h] + tail * mm_nt(v, state_rev)).astype(BF16)
-            ov_ref[0, :, here] = (iv_ref[h] + tail * mm(k, state_rev)).astype(BF16)
-
-    @pl.when(jnp.logical_not(is_target))
-    def _():
-        for o in (oq_ref, ok_ref, ov_ref):
-            o[...] = jnp.zeros_like(o)
+
+    @pl.when(jnp.logical_and(is_target, jnp.logical_not(last_first)))
+    def _():
+        sibling_part(heads - 1)
+        up_local_copy(heads - 1).start()
+
+    @pl.when(jnp.logical_and(is_target, jnp.logical_not(late_states)))
+    def _():
+        for h in range(heads - 1):
+            result(h)
+
+    @pl.when(jnp.logical_and(is_target, jnp.logical_not(last_first)))
+    def _():
+        inner_part(heads - 1)
 
     @pl.when(is_source)
     def _():
         tot_copy().wait_send()
-        for h in range(heads):
-            x_copy(h).wait_send()
+        x_copy().wait_send()
         for d in range(1, n_far + 1):
 
             @pl.when(d <= n_partner)
             def _():
                 tot_far(d).wait_send()
-                for h in range(heads):
-                    agg_far(d, h).wait_send()
+                agg_far(d).wait_send()
 
         ld_copy().wait_send()
         for h in range(heads):
@@ -500,11 +546,26 @@
                 y_copy(i, h).wait_send()
             st_copy(h).wait_send()
 
+    @pl.when(jnp.logical_and(is_target, late_states))
+    def _():
+        for h in range(heads - 1):
+            result(h)
+
     @pl.when(is_target)
     def _():
+        result(heads - 1)
         up_tot_copy().wait_send()
         for h in range(heads):
             up_local_copy(h).wait_send()
+
+    @pl.when(jnp.logical_not(is_target))
+    def _():
+        for o in (oq_ref, ok_ref, ov_ref):
+            o[...] = jnp.zeros_like(o)
+
+    @pl.when(is_target)
+    def _():
+        for h in range(heads):
             up_state_copy(h).wait_send()
 
 
@@ -531,7 +592,7 @@
     vmem = pl.BlockSpec(memory_space=pltpu.VMEM)
     shapes = [jax.ShapeDtypeStruct(queries.shape, BF16)] * 3
     results = pl.pallas_call(
-        functools.partial(kernel, n_pipe, n_chip),
+        functools.partial(kernel, n_pipe, n_chip, n_chip // 2),
         out_shape=shapes,
         in_specs=[pl.BlockSpec(memory_space=pltpu.HBM)] * 5,
         out_specs=[vmem] * 3,
@@ -542,7 +603,6 @@
             pltpu.VMEM((8, length), F32),
             *[pltpu.VMEM(tile, F32)] * 3,
             *[pltpu.VMEM((n_far, *tile), F32)] * 2,
-            pltpu.VMEM((heads, length, size), F32),
             pltpu.VMEM((2, heads, size, size), F32),
             pltpu.VMEM((heads, size, size), F32),
             pltpu.VMEM((heads, size, size), BF16),
@@ -557,14 +617,8 @@
             *[pltpu.VMEM(tile, F32)] * 2,
             *[pltpu.VMEM((heads, length, size), F32)] * 5,
             dma((5,)),
-            dma((1,)),
-            dma((1,)),
-            dma((heads,)),
-            dma((heads,)),
-            dma((n_far,)),
-            dma((n_far,)),
-            dma((n_far, heads)),
-            dma((n_far, heads)),
+            *[dma((1,))] * 4,
+            *[dma((n_far,))] * 4,
             dma((1,)),
             dma((1,)),
             dma((4, heads)),

time: 36.1 us -> 35.4 us (0.981); the launches traced: 36 us -> 34.9 us
  Pallas kernels: 35.4 us -> 34.2 us
    pallas_call x1, Pallas kernels: 34.5 us -> 33.3 us  [per_device(): pl.pallas_call(functools.partial(kernel, n_pipe, n_chip, n_chip // 2), ou...]
where the time goes in v4:
time: 35.4 us; the launch traced here: 34.9 us
  Pallas kernels  34.2 us (97%)
  between operations  0.64 us (2%)
    pallas_call x1, Pallas kernels, per_device(): pl.pallas_call(functools.partial(kernel, n_pipe, n_chip, n_chip // 2), ou...  33.3 us
    pallas_call x1, Pallas kernels, per_device(): pl.pallas_call(put_kernel, out_shape=shapes, in_specs=[anywhere] * 3, out...  0.9 us

profile of v4, /device:TPU:1, one launch (start us, length us, event | category | flops | bytes accessed | tf_op | source)
XLA Modules:
  0.0 34.9 jit_solution(10236950483102688165)
XLA Ops:
  0.6 33.3 %shard_map.76 = (bf16[1,256,512]{2,1,0:T(8,128)(2,1)S(1)}, bf16[1,256,512]{2,1,0:T(8,128)(2,1)S(1)}, bf16[1,256,512]{2,1,0:T(8,128)(2,1)S(1)}) custom-call(bf16[1,256,512]{2,1,0:T(8,128)(2,1)} %q_hbm.1, bf16[1,256,512]{2,1,0:T(8,128)(2,1)} %k_hbm.1, bf16[1,256,512]{2,1,0:T(8,128)(2,1)} %v_hbm.1, bf16[1,256,512]{2,1,0:T(8,128)(2,1)} %g_hbm.1, f32[1,4,256]{2,1,0:T(4,128)} %ld_hbm.1), custom_call_target="tpu_custom_call" | custom-call | tf_op jit(solution)/shard_map/pallas_call | solution.py:594
  34.0 0.9 %shard_map.77 = (bf16[1,256,512]{2,1,0:T(8,128)(2,1)}, bf16[1,256,512]{2,1,0:T(8,128)(2,1)}, bf16[1,256,512]{2,1,0:T(8,128)(2,1)}) custom-call(bf16[1,256,512]{2,1,0:T(8,128)(2,1)S(1)} %get-tuple-element.6.a_ref, bf16[1,256,512]{2,1,0:T(8,128)(2,1)S(1)} %get-tuple-element.7.b_ref, bf16[1,256,512]{2,1,0:T(8,128)(2,1)S(1)} %get-tuple-element.8.c_ref), custom_call_target="tpu_custom_call" | custom-call | tf_op jit(solution)/shard_map/pallas_call | solution.py:643

commit v5 on v4

--- a/solution.py
+++ b/solution.py
@@ -508,27 +508,6 @@
         up_local_copy(heads - 1).start()
         inner_part(heads - 1)
 
-    @pl.when(is_target)
-    def _():
-        for h in range(heads):
-            st_copy(h).wait_recv()
-            up_state_copy(h).start()
-        up_tot_copy().wait_recv()
-
-    @pl.when(jnp.logical_and(is_target, jnp.logical_not(last_first)))
-    def _():
-        sibling_part(heads - 1)
-        up_local_copy(heads - 1).start()
-
-    @pl.when(jnp.logical_and(is_target, jnp.logical_not(late_states)))
-    def _():
-        for h in range(heads - 1):
-            result(h)
-
-    @pl.when(jnp.logical_and(is_target, jnp.logical_not(last_first)))
-    def _():
-        inner_part(heads - 1)
-
     @pl.when(is_source)
     def _():
         tot_copy().wait_send()
@@ -541,16 +520,36 @@
                 agg_far(d).wait_send()
 
         ld_copy().wait_send()
-        for h in range(heads):
+        for h in range(heads - 1):
             for i in range(4):
                 y_copy(i, h).wait_send()
-            st_copy(h).wait_send()
-
-    @pl.when(jnp.logical_and(is_target, late_states))
+
+    @pl.when(is_target)
+    def _():
+        for h in range(heads):
+            st_copy(h).wait_recv()
+            up_state_copy(h).start()
+        up_tot_copy().wait_recv()
+
+    @pl.when(jnp.logical_and(is_target, jnp.logical_not(last_first)))
+    def _():
+        sibling_part(heads - 1)
+        up_local_copy(heads - 1).start()
+
+    @pl.when(jnp.logical_and(is_target, jnp.logical_not(late_states)))
     def _():
         for h in range(heads - 1):
             result(h)
 
+    @pl.when(jnp.logical_and(is_target, jnp.logical_not(last_first)))
+    def _():
+        inner_part(heads - 1)
+
+    @pl.when(jnp.logical_and(is_target, late_states))
+    def _():
+        for h in range(heads - 1):
+            result(h)
+
     @pl.when(is_target)
     def _():
         result(heads - 1)
@@ -567,6 +566,13 @@
     def _():
         for h in range(heads):
             up_state_copy(h).wait_send()
+
+    @pl.when(is_source)
+    def _():
+        for i in range(4):
+            y_copy(i, heads - 1).wait_send()
+        for h in range(heads):
+            st_copy(h).wait_send()
 
 
 def put_kernel(a_ref, b_ref, c_ref, oa_ref, ob_ref, oc_ref, sem):

time: 35.4 us -> 35.3 us (level)
  no operation moved by 1% of the time
where the time goes in v5:
time: 35.3 us; the launch traced here: 34.9 us
  Pallas kernels  34.3 us (97%)
  between operations  0.64 us (2%)
    pallas_call x1, Pallas kernels, per_device(): pl.pallas_call(functools.partial(kernel, n_pipe, n_chip, n_chip // 2), ou...  33.4 us
    pallas_call x1, Pallas kernels, per_device(): pl.pallas_call(put_kernel, out_shape=shapes, in_specs=[anywhere] * 3, out...  0.9 us

profile of v5, /device:TPU:1, one launch (start us, length us, event | category | flops | bytes accessed | tf_op | source)
XLA Modules:
  0.0 34.9 jit_solution(8184305005944993149)
XLA Ops:
  0.6 33.4 %shard_map.76 = (bf16[1,256,512]{2,1,0:T(8,128)(2,1)S(1)}, bf16[1,256,512]{2,1,0:T(8,128)(2,1)S(1)}, bf16[1,256,512]{2,1,0:T(8,128)(2,1)S(1)}) custom-call(bf16[1,256,512]{2,1,0:T(8,128)(2,1)} %q_hbm.1, bf16[1,256,512]{2,1,0:T(8,128)(2,1)} %k_hbm.1, bf16[1,256,512]{2,1,0:T(8,128)(2,1)} %v_hbm.1, bf16[1,256,512]{2,1,0:T(8,128)(2,1)} %g_hbm.1, f32[1,4,256]{2,1,0:T(4,128)} %ld_hbm.1), custom_call_target="tpu_custom_call" | custom-call | tf_op jit(solution)/shard_map/pallas_call | solution.py:600
  34.0 0.9 %shard_map.77 = (bf16[1,256,512]{2,1,0:T(8,128)(2,1)}, bf16[1,256,512]{2,1,0:T(8,128)(2,1)}, bf16[1,256,512]{2,1,0:T(8,128)(2,1)}) custom-call(bf16[1,256,512]{2,1,0:T(8,128)(2,1)S(1)} %get-tuple-element.6.a_ref, bf16[1,256,512]{2,1,0:T(8,128)(2,1)S(1)} %get-tuple-element.7.b_ref, bf16[1,256,512]{2,1,0:T(8,128)(2,1)S(1)} %get-tuple-element.8.c_ref), custom_call_target="tpu_custom_call" | custom-call | tf_op jit(solution)/shard_map/pallas_call | solution.py:649
